TPU v7x, 128 devices: a whole 4x4x4 slice. The times are simulated.
128 devices in a mesh: gx: 16 (over z, y_lo, core), gy: 8 (over x, y_hi).
Axes of the slice: x: 4, y: 4 (y_hi: 2, y_lo: 2; y = y_hi * 2 + y_lo), z: 4, core: 2. Of those that a mesh axis runs over, the one named last changes fastest.
Arguments:
- velocity: float32 [3, 4096, 1024], P(None, 'gx', 'gy'), may hold values from 0.4 to 1.6
- adjoint_seed: float32 [3, 4096, 1024], P(None, 'gx', 'gy'), may hold values from -6 to 6
- courant: float32 [3, 4096, 1024], P(None, 'gx', 'gy'), may hold values from 0.1 to 0.45
- viscosity: float32 [3, 4096, 1024], P(None, 'gx', 'gy'), may hold values from 0.02 to 0.1
- turbine_tile: int32 [512, 1], P(('gx', 'gy')), may hold values from 0 to 127; in each aligned block of 512 rows (0 to 511, 512 to 1023, ...) at most 12 rows name the same one
- turbine_offset: int32 [512, 2], P(('gx', 'gy')), may hold values from 0 to 64
- thrust: float32 [512], P(('gx', 'gy')), may hold values from 0.5 to 2
- disk_width: float32 [512], P(('gx', 'gy')), may hold values from 8 to 16
Outputs:
- adjoint_start: float32 [3, 4096, 1024], P(None, 'gx', 'gy')
- thrust_grad: float32 [512], P(('gx', 'gy'))
Inputs may be any that keep to these rules, and one draw needn't show every extreme that they name: `turbine_tile`: each turbine's tile is the index along gx times the number of devices of gy plus the index along gy of the device whose cells hold its footprint. No tile holds more than 12 turbines, and some tile holds exactly 12.
All inputs are finite; a program needn't handle non-finite values.
Results may differ from a plain program's by a relative error of at most 0.00002.
Values sent between devices are 32-bit elements; how exact they have to be, the bound alone decides.
A program may use at most 128 MiB of HBM per device.

v0:
```python
import jax
import jax.numpy as jnp
from jax import lax
from jax.sharding import PartitionSpec as P

LEV = 3
STEPS = 8
FP = 64
VERTICAL_MIX = 0.05
DRAG_SCALE = 0.01


def padded_2(block, sides, width):
    for axis, dim in sides:
        count = lax.axis_size(axis)
        forward = [(i, i + 1) for i in range(count - 1)]
        forward.append((count - 1, 0))
        backward = [(target, source) for source, target in forward]
        low = lax.ppermute(
            lax.slice_in_dim(block, block.shape[dim] - width, None, axis=dim), axis, forward
        )
        high = lax.ppermute(lax.slice_in_dim(block, 0, width, axis=dim), axis, backward)
        block = jnp.concatenate([low, block, high], axis=dim)
    return block


def drag_law(state):
    return state * jnp.sqrt(state * state + 1.0)


def drag_slope(state):
    square_one = state * state + 1.0
    return (square_one + state * state) / jnp.sqrt(square_one)


def vertical(center):
    zero_row = jnp.zeros_like(center[:1])
    from_above = jnp.concatenate([center[1:] - center[:-1], zero_row], axis=0)
    from_below = jnp.concatenate([zero_row, center[:-1] - center[1:]], axis=0)
    return from_above + from_below


def advance(padded, advect, diffuse, drag_coef):
    center = padded[:, 1:-1, 1:-1]
    upwind = padded[:, :-2, 1:-1]
    downwind = padded[:, 2:, 1:-1]
    left_cell = padded[:, 1:-1, :-2]
    right_cell = padded[:, 1:-1, 2:]
    return (
        center
        + advect * (upwind - center)
        + diffuse * (downwind + upwind + right_cell + left_cell - 4.0 * center)
        + VERTICAL_MIX * vertical(center)
        - drag_coef * drag_law(center)
    )


def retreat(padded, advect_ext, diffuse_ext, drag_coef, state):
    flux_adv = advect_ext * padded
    flux_dif = diffuse_ext * padded
    center = padded[:, 1:-1, 1:-1]
    return (
        center
        - flux_adv[:, 1:-1, 1:-1]
        - 4.0 * flux_dif[:, 1:-1, 1:-1]
        + flux_adv[:, 2:, 1:-1]
        + (
            flux_dif[:, 2:, 1:-1]
            + flux_dif[:, :-2, 1:-1]
            + flux_dif[:, 1:-1, 2:]
            + flux_dif[:, 1:-1, :-2]
        )
        + VERTICAL_MIX * vertical(center)
        - drag_coef * drag_slope(state) * center
    )


def footprint(disk_width):
    cell_pos = jnp.arange(FP, dtype=jnp.float32) - (FP - 1) / 2.0
    profile = jnp.exp(
        -(cell_pos[None, :] * cell_pos[None, :]) / (2.0 * disk_width[:, None] * disk_width[:, None])
    )
    level_pos = jnp.arange(LEV, dtype=jnp.float32) - (LEV - 1) / 2.0
    level_gain = DRAG_SCALE * jnp.exp(-0.5 * level_pos * level_pos)
    return level_gain[None, :, None, None] * profile[:, None, :, None] * profile[:, None, None, :]


def extend_rim(array, rim_depth):
    return padded_2(array, (("gx", 1), ("gy", 2)), rim_depth)


def trim_rim(array, stored_margin, wanted):
    excess = stored_margin - wanted
    if excess == 0:
        return array
    return array[:, excess:-excess, excess:-excess]


def coef_at(coef_ext, coef_margin, wanted, levels):
    portion = trim_rim(coef_ext, coef_margin, wanted)
    return (portion[:levels], portion[levels : 2 * levels], portion[2 * levels : 3 * levels])


def shards(
    velocity, adjoint_seed, courant, viscosity, turbine_tile, turbine_offset, thrust, disk_width
):
    levels = velocity.shape[0]
    places, shifts = (
        lax.all_gather(turbine_tile, ("gx", "gy"), axis=0, tiled=True),
        lax.all_gather(turbine_offset, ("gx", "gy"), axis=0, tiled=True),
    )
    thrusts, widths = (
        lax.all_gather(thrust, ("gx", "gy"), axis=0, tiled=True),
        lax.all_gather(disk_width, ("gx", "gy"), axis=0, tiled=True),
    )
    turbine_count = places.shape[0]
    own_index = lax.axis_index("gx") * lax.axis_size("gy") + lax.axis_index("gy")
    turbine_ids = jnp.arange(turbine_count, dtype=jnp.int32)
    in_tile = places[:, 0] == own_index
    sort_keys = jnp.where(in_tile, turbine_ids, turbine_ids + turbine_count)
    slot_count = 3 * thrust.shape[0]
    slot_ids = jnp.argsort(sort_keys)[:slot_count]
    slot_match = in_tile[slot_ids]
    slot_live = slot_match.astype(jnp.float32)
    slot_rows = shifts[slot_ids, 0]
    slot_cols = shifts[slot_ids, 1]
    kernels = footprint(widths[slot_ids])
    slot_thrust = thrusts[slot_ids] * slot_live

    def add_turbine(slot_index, field_now):
        corner = (jnp.int32(0), slot_rows[slot_index], slot_cols[slot_index])
        block_vals = lax.dynamic_slice(field_now, corner, (levels, FP, FP))
        return lax.dynamic_update_slice(
            field_now, block_vals + slot_thrust[slot_index] * kernels[slot_index], corner
        )

    drag_field = lax.fori_loop(0, slot_count, add_turbine, jnp.zeros_like(velocity))
    forward_depth = 1
    coef_margin = 1
    coef_margin = forward_depth
    coef_ext = extend_rim(jnp.concatenate([courant, viscosity, drag_field], axis=0), forward_depth)
    state = velocity
    state_margin = 0
    states = []
    for step_index in range(STEPS):
        if step_index + 1 < STEPS and state_margin == 0:
            state = extend_rim(state, forward_depth)
            state_margin = forward_depth
        states.append((state, state_margin))
        if step_index + 1 < STEPS:
            advect, diffuse, drag_coef = coef_at(coef_ext, coef_margin, state_margin - 1, levels)
            state = advance(state, advect, diffuse, drag_coef)
            state_margin = state_margin - 1
    adjoint = adjoint_seed
    adjoint_margin = 0
    sensitivity = jnp.zeros_like(velocity)
    for step_index in reversed(range(STEPS)):
        stored, stored_margin = states[step_index]
        sensitivity = sensitivity - trim_rim(adjoint, adjoint_margin, 0) * drag_law(
            trim_rim(stored, stored_margin, 0)
        )
        adjoint = extend_rim(adjoint, forward_depth)
        adjoint_margin = forward_depth
        advect_ext, diffuse_ext, unused_drag = coef_at(
            coef_ext, coef_margin, adjoint_margin, levels
        )
        unused_adv, unused_dif, drag_mid = coef_at(
            coef_ext, coef_margin, adjoint_margin - 1, levels
        )
        adjoint = retreat(
            adjoint,
            advect_ext,
            diffuse_ext,
            drag_mid,
            trim_rim(stored, stored_margin, adjoint_margin - 1),
        )
        adjoint_margin = adjoint_margin - 1
    adjoint_start = trim_rim(adjoint, adjoint_margin, 0)

    def slot_total(row_first, col_first, kernel):
        block_vals = lax.dynamic_slice(
            sensitivity, (jnp.int32(0), row_first, col_first), (levels, FP, FP)
        )
        return jnp.sum(kernel * block_vals)

    totals = jax.vmap(slot_total)(slot_rows, slot_cols, kernels)
    values = thrusts[slot_ids] * totals * slot_live
    one_hot = (turbine_ids[None, :] == slot_ids[:, None]).astype(jnp.float32)
    spread = jnp.sum(one_hot * values[:, None], axis=0)
    return (adjoint_start, lax.psum_scatter(spread, ("gx", "gy"), scatter_dimension=0, tiled=True))


def solution(mesh):
    placed = (
        P(None, "gx", "gy"),
        P(None, "gx", "gy"),
        P(None, "gx", "gy"),
        P(None, "gx", "gy"),
        P(("gx", "gy"), None),
        P(("gx", "gy"), None),
        P(("gx", "gy")),
        P(("gx", "gy")),
    )
    return jax.shard_map(
        shards,
        mesh=mesh,
        in_specs=placed,
        out_specs=(P(None, "gx", "gy"), P(("gx", "gy"))),
        check_vma=False,
    )
```

profile of v0, /device:TPU:1, one launch (start us, length us, event | category | flops | bytes accessed | tf_op | source)
XLA Modules:
  0.0 1061.2 jit_solution(10426289407377339527)
XLA Ops:
  6.1 69.8 %all-reduce.32 = s32[512]{0:T(512)S(1)} all-reduce(s32[512]{0:T(512)S(1)} %bitcast_dynamic-update-slice_fusion.1), channel_id=1, replica_groups=mesh['gx'=16,'gy'=8] {'gx','gy'}, use_global_device_ids=true, to_apply=%add.32 | all-reduce | flops 512 | bytes 4096
  75.9 3.8 sort.17
  80.3 303.1 %all-gather = s32[128,4,2]{1,2,0:T(2,128)S(1)} all-gather(s32[1,4,2]{1,2,0:T(2,128)} %bitcast.32), channel_id=1, replica_groups=mesh['gx'=16,'gy'=8] {'gx','gy'}, dimensions={0}, use_global_device_ids=true | all-gather | bytes 4128 | tf_op jit(solution)/shard_map/all_gather | solution.py:110
  386.2 71.6 %all-reduce.36 = (f32[512]{0:T(512)S(1)}, f32[512]{0:T(512)S(1)}) all-reduce(f32[512]{0:T(512)S(1)} %dynamic-update-slice.3, f32[512]{0:T(512)S(1)} %dynamic-update-slice.4), channel_id=1, replica_groups=mesh['gx'=16,'gy'=8] {'gx','gy'}, use_global_device_ids=true, to_apply=%add.33 | all-reduce | flops 1024 | bytes 8192
  460.0 99.8 %while.14 = (s32[]{:T(128)}, f32[3,256,128]{2,1,0:T(8,128)S(1)}, s32[12]{0:T(128)S(1)}, s32[12]{0:T(128)S(1)}, f32[12]{0:T(128)S(1)}, /*index=5*/f32[12,3,64,64]...) while((s32[]{:T(128)}, f32[3,256,128]{2,1,0:T(8,128)S(1)}, s32[12]{0:T(128)S(1)}, ...), condition=%wide.region_2.3_spmd, body=%wide.region_1.2_spmd.sunk | while | flops 24584 | bytes 245993 | solution.py:137
  578.1 4.5 collective-permute-start.14
  584.9 6.0 fusion.113
  591.0 4.8 collective-permute-start.17
  602.0 5.0 collective-permute-start.18
  609.3 5.9 fusion.102
  632.9 5.9 fusion.91
  638.9 5.9 collective-permute-start.25
  645.2 4.7 collective-permute-start.7
  653.1 5.1 collective-permute-start.26
  660.6 6.0 fusion.80
  674.3 5.0 collective-permute-start.30
  682.3 5.0 fusion.69
  699.8 3.9 collective-permute-start.34
  725.1 5.1 fusion.131
  730.4 4.9 fusion.130
  735.4 4.1 fusion.121
  739.6 5.7 collective-permute-start.37
  751.4 4.7 collective-permute-start.39
  770.8 6.0 collective-permute-start.41
  798.2 5.3 collective-permute-start.45
  825.1 5.3 collective-permute-start.49
  852.0 5.3 collective-permute-start.53
  880.4 5.3 collective-permute-start.57
  906.6 9.2 multiply_subtract_fusion
  916.8 5.4 collective-permute-start.61
  923.2 49.5 %while.15 = (s32[]{:T(128)}, f32[3,256,128]{2,1,0:T(8,128)}, s32[12,3]{0,1:T(4,128)}, f32[12,3,64,64]{3,2,1,0:T(8,128)}, s32[]{:T(128)}) while((s32[]{:T(128)}, f32[3,256,128]{2,1,0:T(8,128)}, s32[12,3]{0,1:T(4,128)}, f32[12,3,64,64]{3,2,1,0:T(8,128)}, s32[]{:T(128)}) %tuple.129), condition=%wide.while_cond, body=%wide.while_body.sunk | while | flops 2 | bytes 197749 | solution.py:181
  985.3 65.9 %all-reduce.35 = f32[512]{0:T(512)} all-reduce(f32[512]{0:T(512)} %select_reduce_fusion), channel_id=2, replica_groups=mesh['gx'=16,'gy'=8] {'gx','gy'}, use_global_device_ids=true, to_apply=%region_5.6.clone | all-reduce | flops 512 | bytes 4096
  (602 shorter events, 363.2 us)
Async XLA Ops:
  1.4 559.4 %collective-permute-start.9 = (f32[3,1,128]{2,1,0:T(1,128)S(1)}, f32[3,1,128]{2,1,0:T(1,128)S(1)}, u32[]{:S(2)}, u32[]{:S(2)}) collective-permute-start(f32[3,1,128]{2,1,0:T(1,128)S(1)} %get-tuple-element.326), channel_id=1, source_target_pairs={{8,0},{16,8},{24,16},{32,24},{40,32},{48,40},{56,48},{64,56},{72,6... | collective-permute-start | bytes 4616 | tf_op jit(solution)/shard_map/ppermute | solution.py:22
  2.8 558.0 %collective-permute-start.8 = (f32[3,1,128]{2,1,0:T(1,128)S(1)}, f32[3,1,128]{2,1,0:T(1,128)S(1)}, u32[]{:S(2)}, u32[]{:S(2)}) collective-permute-start(f32[3,1,128]{2,1,0:T(1,128)S(1)} %get-tuple-element.327), channel_id=1, source_target_pairs={{0,8},{8,16},{16,24},{24,32},{32,40},{40,48},{48,56},{56,64},{64,7... | collective-permute-start | bytes 4616 | tf_op jit(solution)/shard_map/ppermute | solution.py:19
  576.9 6.6 collective-permute-start.15
  591.0 7.7 collective-permute-start.17
  595.8 22.9 %collective-permute-start.5 = (f32[3,1,128]{2,1,0:T(1,128)S(1)}, f32[3,1,128]{2,1,0:T(1,128)S(1)}, u32[]{:S(2)}, u32[]{:S(2)}) collective-permute-start(f32[3,1,128]{2,1,0:T(1,128)S(1)} %get-tuple-element.329), channel_id=1, source_target_pairs={{8,0},{16,8},{24,16},{32,24},{40,32},{48,40},{56,48},{64,56},{72,6... | collective-permute-start | bytes 4616 | tf_op jit(solution)/shard_map/ppermute | solution.py:22
  596.4 22.9 %collective-permute-start.4 = (f32[3,1,128]{2,1,0:T(1,128)S(1)}, f32[3,1,128]{2,1,0:T(1,128)}, u32[]{:S(2)}, u32[]{:S(2)}) collective-permute-start(f32[3,1,128]{2,1,0:T(1,128)S(1)} %get-tuple-element.328), channel_id=1, source_target_pairs={{0,8},{8,16},{16,24},{24,32},{32,40},{40,48},{48,56},{56,64},{64,7... | collective-permute-start | bytes 4616 | tf_op jit(solution)/shard_map/ppermute | solution.py:19
  601.3 6.6 collective-permute-start.19
  624.7 6.7 collective-permute-start.23
  638.9 11.3 %collective-permute-start.25 = (f32[3,1,128]{2,0,1:T(4,128)S(1)}, f32[3,1,128]{2,0,1:T(4,128)S(1)}, u32[]{:S(2)}, u32[]{:S(2)}) collective-permute-start(f32[3,1,128]{2,0,1:T(4,128)S(1)} %get-tuple-element.299), channel_id=1, source_target_pairs={{8,0},{16,8},{24,16},{32,24},{40,32},{48,40},{56,48},{64,56},{72,6... | collective-permute-start | bytes 4616 | tf_op jit(solution)/shard_map/ppermute | solution.py:22
  645.2 25.3 %collective-permute-start.7 = (f32[3,258,1]{1,0,2:T(4,128)S(1)}, f32[3,258,1]{1,0,2:T(4,128)S(1)}, u32[]{:S(2)}, u32[]{:S(2)}) collective-permute-start(f32[3,258,1]{1,0,2:T(4,128)S(1)} %copy.743), channel_id=1, source_target_pairs={{1,0},{2,1},{3,2},{4,3},{5,4},{6,5},{7,6},{0,7},{9,8},{10,9},{11,1... | collective-permute-start | bytes 9296 | tf_op jit(solution)/shard_map/ppermute | solution.py:22
  650.1 21.5 %collective-permute-start.6 = (f32[3,258,1]{1,0,2:T(4,128)S(1)}, f32[3,258,1]{1,0,2:T(4,128)S(1)}, u32[]{:S(2)}, u32[]{:S(2)}) collective-permute-start(f32[3,258,1]{1,0,2:T(4,128)S(1)} %copy.742), channel_id=1, source_target_pairs={{0,1},{1,2},{2,3},{3,4},{4,5},{5,6},{6,7},{7,0},{8,9},{9,10},{10,1... | collective-permute-start | bytes 9296 | tf_op jit(solution)/shard_map/ppermute | solution.py:19
  673.5 6.6 collective-permute-start.31
  674.3 7.0 collective-permute-start.30
  690.7 12.9 %collective-permute-start.1 = (f32[9,1,128]{2,0,1:T(8,128)S(1)}, f32[9,1,128]{2,0,1:T(8,128)S(1)}, u32[]{:S(2)}, u32[]{:S(2)}) collective-permute-start(f32[9,1,128]{2,0,1:T(8,128)S(1)} %get-tuple-element.233), channel_id=1, source_target_pairs={{8,0},{16,8},{24,16},{32,24},{40,32},{48,40},{56,48},{64,56},{72,6... | collective-permute-start | bytes 13832 | tf_op jit(solution)/shard_map/ppermute | solution.py:22
  692.7 11.0 %collective-permute-start = (f32[9,1,128]{2,0,1:T(8,128)S(1)}, f32[9,1,128]{2,0,1:T(8,128)S(1)}, u32[]{:S(2)}, u32[]{:S(2)}) collective-permute-start(f32[9,1,128]{2,0,1:T(8,128)S(1)} %get-tuple-element.232), channel_id=1, source_target_pairs={{0,8},{8,16},{16,24},{24,32},{32,40},{40,48},{48,56},{56,64},{64,7... | collective-permute-start | bytes 13832 | tf_op jit(solution)/shard_map/ppermute | solution.py:19
  696.6 19.7 %collective-permute-start.35 = (f32[3,258,1]{1,0,2:T(4,128)S(1)}, f32[3,258,1]{1,0,2:T(4,128)}, u32[]{:S(2)}, u32[]{:S(2)}) collective-permute-start(f32[3,258,1]{1,0,2:T(4,128)S(1)} %copy.698), channel_id=1, source_target_pairs={{0,1},{1,2},{2,3},{3,4},{4,5},{5,6},{6,7},{7,0},{8,9},{9,10},{10,1... | collective-permute-start | bytes 9296 | tf_op jit(solution)/shard_map/ppermute | solution.py:19
  699.8 18.3 %collective-permute-start.34 = (f32[3,258,1]{1,0,2:T(4,128)}, f32[3,258,1]{1,0,2:T(4,128)}, u32[]{:S(2)}, u32[]{:S(2)}) collective-permute-start(f32[3,258,1]{1,0,2:T(4,128)} %copy.696), channel_id=1, source_target_pairs={{1,0},{2,1},{3,2},{4,3},{5,4},{6,5},{7,6},{0,7},{9,8},{10,9},{11,1... | collective-permute-start | bytes 9296 | tf_op jit(solution)/shard_map/ppermute | solution.py:22
  709.5 10.4 collective-permute-start.3
  714.8 7.7 collective-permute-start.2
  751.4 9.3 collective-permute-start.39
  758.0 6.8 collective-permute-start.38
  770.8 6.8 collective-permute-start.41
  782.0 7.1 collective-permute-start.43
  808.8 7.3 collective-permute-start.47
  835.7 7.1 collective-permute-start.51
  862.6 7.3 collective-permute-start.55
  866.3 6.6 collective-permute-start.54
  891.5 7.2 collective-permute-start.59
  916.8 58.3 %collective-permute-start.61 = (f32[3,1,128]{2,0,1:T(4,128)}, f32[3,1,128]{2,0,1:T(4,128)}, u32[]{:S(2)}, u32[]{:S(2)}) collective-permute-start(f32[3,1,128]{2,0,1:T(4,128)} %get-tuple-element.263), channel_id=1, source_target_pairs={{8,0},{16,8},{24,16},{32,24},{40,32},{48,40},{56,48},{64,56},{72,6... | collective-permute-start | bytes 4616 | tf_op jit(solution)/shard_map/ppermute | solution.py:22
  922.2 52.9 %collective-permute-start.60 = (f32[3,1,128]{2,0,1:T(4,128)}, f32[3,1,128]{2,0,1:T(4,128)}, u32[]{:S(2)}, u32[]{:S(2)}) collective-permute-start(f32[3,1,128]{2,0,1:T(4,128)} %get-tuple-element.262), channel_id=1, source_target_pairs={{0,8},{8,16},{16,24},{24,32},{32,40},{40,48},{48,56},{56,64},{64,7... | collective-permute-start | bytes 4616 | tf_op jit(solution)/shard_map/ppermute | solution.py:19
  979.1 73.3 %collective-permute-start.63 = (f32[3,258,1]{1,0,2:T(4,128)}, f32[3,258,1]{1,0,2:T(4,128)}, u32[]{:S(2)}, u32[]{:S(2)}) collective-permute-start(f32[3,258,1]{1,0,2:T(4,128)} %copy.735), channel_id=1, source_target_pairs={{1,0},{2,1},{3,2},{4,3},{5,4},{6,5},{7,6},{0,7},{9,8},{10,9},{11,1... | collective-permute-start | bytes 9296 | tf_op jit(solution)/shard_map/ppermute | solution.py:22
  982.9 71.3 %collective-permute-start.62 = (f32[3,258,1]{1,0,2:T(4,128)}, f32[3,258,1]{1,0,2:T(4,128)}, u32[]{:S(2)}, u32[]{:S(2)}) collective-permute-start(f32[3,258,1]{1,0,2:T(4,128)} %copy.734), channel_id=1, source_target_pairs={{0,1},{1,2},{2,3},{3,4},{4,5},{5,6},{6,7},{7,0},{8,9},{9,10},{10,1... | collective-permute-start | bytes 9296 | tf_op jit(solution)/shard_map/ppermute | solution.py:19
  (138 other events, 1412.9 us)
where the time goes:
time: 1070 us; the launch traced here: 1060 us
  blocking collectives  510 us (48%)
  local copies, waits for them, and re-layouts  218 us (20%)
  starting transfers between devices  135 us (13%)
  other arithmetic  128 us (12%)
  loops' own time  47.1 us (4%)
  waiting for transfers between devices  19.6 us (2%)
    all_gather x1, blocking collectives, shards(): lax.all_gather(turbine_offset, ('gx', 'gy'), axis=0, tiled=True)  303 us
    unnamed x3, blocking collectives  207 us
    ppermute x32, starting transfers between devices, padded_2(): lax.ppermute(lax.slice_in_dim(block, 0, width, axis=dim), axis, backward)  116 us
    gather x36, local copies, waits for them, and re-layouts  49.5 us
    another operation x1, loops' own time, shards(): lax.fori_loop(0, slot_count, add_turbine, jnp.zeros_like(velocity))  47 us
    slice x37, local copies, waits for them, and re-layouts, padded_2(): lax.slice_in_dim(block, block.shape[dim] - width, None, axis=dim)  34.9 us
    sub x6, other arithmetic, advance(): center + advect * (upwind - center)  32.3 us
    slice x22, local copies, waits for them, and re-layouts, padded_2(): lax.slice_in_dim(block, 0, width, axis=dim)  25.5 us
  transfers between devices with their start and end apart: 64, of which 22 were waited for; matrix products, arithmetic and copies ran while one was open for 20% of the time, Pallas kernels for 0%

commit v1 on v0

--- a/solution.py
+++ b/solution.py
@@ -107,7 +107,12 @@
     levels = velocity.shape[0]
     places, shifts = (
         lax.all_gather(turbine_tile, ("gx", "gy"), axis=0, tiled=True),
-        lax.all_gather(turbine_offset, ("gx", "gy"), axis=0, tiled=True),
+        jnp.concatenate(
+            lax.all_to_all(
+                jnp.stack([turbine_offset] * lax.axis_size(("gx", "gy"))), ("gx", "gy"), 0, 0
+            ),
+            axis=0,
+        ),
     )
     thrusts, widths = (
         lax.all_gather(thrust, ("gx", "gy"), axis=0, tiled=True),

time: 1070 us -> 786 us (0.73)
  blocking collectives: 510 us -> 195 us
  local copies, waits for them, and re-layouts: 218 us -> 234 us
    all_gather x1 -> x0, blocking collectives: 303 us -> none  [shards(): lax.all_gather(turbine_offset, ('gx', 'gy'), axis=0, tiled=True)]
    dynamic_slice x24, local copies, waits for them, and re-layouts: 14.1 us -> 30.4 us  [add_turbine(): corner = (jnp.int32(0), slot_rows[slot_index], slot_cols[slot_index])]
    all_to_all x0 -> x1, starting transfers between devices: none -> 11.9 us  [shards(): lax.all_to_all(jnp.stack([turbine_offset] * lax.axis_size(('gx', 'gy'))),...]
    unnamed x3, blocking collectives: 207 us -> 195 us
  transfers between devices with their start and end apart: 64 -> 65, of which waited for: 22 -> 19; matrix products, arithmetic and copies ran while one was open for 20% -> 30% of each run, Pallas kernels for 0% -> 0%
where the time goes in v1:
time: 786 us; the launch traced here: 773 us
  local copies, waits for them, and re-layouts  234 us (30%)
  blocking collectives  195 us (25%)
  starting transfers between devices  145 us (18%)
  other arithmetic  128 us (16%)
  loops' own time  50.1 us (6%)
  waiting for transfers between devices  18.6 us (2%)
    unnamed x3, blocking collectives  195 us
    ppermute x32, starting transfers between devices, padded_2(): lax.ppermute(lax.slice_in_dim(block, 0, width, axis=dim), axis, backward)  116 us
    another operation x1, loops' own time, shards(): lax.fori_loop(0, slot_count, add_turbine, jnp.zeros_like(velocity))  50 us
    gather x36, local copies, waits for them, and re-layouts  43.4 us
    slice x37, local copies, waits for them, and re-layouts, padded_2(): lax.slice_in_dim(block, block.shape[dim] - width, None, axis=dim)  32.8 us
    sub x6, other arithmetic, advance(): center + advect * (upwind - center)  32.4 us
    dynamic_slice x24, local copies, waits for them, and re-layouts, add_turbine(): corner = (jnp.int32(0), slot_rows[slot_index], slot_cols[slot_index])  30.4 us
    slice x22, local copies, waits for them, and re-layouts, padded_2(): lax.slice_in_dim(block, 0, width, axis=dim)  25.7 us
  transfers between devices with their start and end apart: 65, of which 19 were waited for; matrix products, arithmetic and copies ran while one was open for 30% of the time, Pallas kernels for 0%

profile of v1, /device:TPU:1, one launch (start us, length us, event | category | flops | bytes accessed | tf_op | source)
XLA Modules:
  0.0 773.5 jit_solution(12534742921013164514)
XLA Ops:
  5.5 11.9 %all-to-all-start = ((s32[128,4,2]{1,2,0:T(2,128)}), s32[128,4,2]{1,2,0:T(2,128)S(1)}, u32[]{:S(2)}, u32[]{:S(2)}) async-start(s32[128,4,2]{1,2,0:T(2,128)} %stack.2), calls=%async_computation | async-start | bytes 262144 | tf_op jit(solution)/shard_map/all_to_all | solution.py:111
  19.7 67.1 %all-reduce.32 = s32[512]{0:T(512)S(1)} all-reduce(s32[512]{0:T(512)S(1)} %bitcast_dynamic-update-slice_fusion.1), channel_id=1, replica_groups=mesh['gx'=16,'gy'=8] {'gx','gy'}, use_global_device_ids=true, to_apply=%add.32 | all-reduce | flops 512 | bytes 4096
  92.3 62.6 %all-reduce.36 = (f32[512]{0:T(512)S(1)}, f32[512]{0:T(512)S(1)}) all-reduce(f32[512]{0:T(512)S(1)} %dynamic-update-slice.3, f32[512]{0:T(512)S(1)} %dynamic-update-slice.4), channel_id=1, replica_groups=mesh['gx'=16,'gy'=8] {'gx','gy'}, use_global_device_ids=true, to_apply=%add.33 | all-reduce | flops 1024 | bytes 8192
  170.1 120.6 %while.14 = (s32[]{:T(128)}, f32[3,256,128]{2,1,0:T(8,128)S(1)}, s32[12]{0:T(128)}, s32[12]{0:T(128)}, f32[12]{0:T(128)S(1)}, /*index=5*/f32[12,3,64,64]{3,2,1,0...) while((s32[]{:T(128)}, f32[3,256,128]{2,1,0:T(8,128)S(1)}, s32[12]{0:T(128)}, s32[12]{0:T(128)}, ...), condition=%wide.region_2.3_spmd, body=%wide.region_1.2_spmd.sunk | while | flops 24584 | bytes 245993 | solution.py:142
  303.4 4.4 collective-permute-start.14
  310.1 6.0 fusion.113
  316.1 4.0 collective-permute-start.17
  327.4 4.0 collective-permute-start.18
  333.7 5.9 fusion.102
  350.5 4.4 collective-permute-start.22
  357.3 5.9 fusion.91
  363.3 5.2 collective-permute-start.25
  369.0 5.4 collective-permute-start.7
  377.6 5.1 collective-permute-start.26
  385.0 6.0 fusion.80
  398.3 5.4 collective-permute-start.30
  406.8 5.0 fusion.69
  423.0 5.1 collective-permute-start.34
  449.6 5.1 fusion.131
  454.8 4.9 fusion.130
  459.9 4.1 fusion.121
  464.0 5.7 collective-permute-start.37
  475.8 4.7 collective-permute-start.39
  495.2 6.0 collective-permute-start.41
  522.8 5.3 collective-permute-start.45
  551.1 5.2 collective-permute-start.49
  578.3 5.3 collective-permute-start.53
  605.8 4.9 collective-permute-start.57
  631.1 9.2 %multiply_subtract_fusion = (f32[3,256,128]{2,0,1:T(4,128)S(1)}, f32[3,256,128]{2,0,1:T(4,128)S(1)}) fusion(f32[3,256,128]{2,0,1:T(4,128)} %copy-done.41, f32[3,256,128]{2,0,1:T(4,128)S(1)} %copy-done.18, f32[3,256,128]{2,0,1:T(4,128)S(1)} %copy-done.15, f32[3,256,128]{2,0,1:T(4,128)S(1)} %copy-done.12, f32[3,256,128]{2,0,1:T(4,128)S(1)} %copy-done.9, ...), kind=kLoop, calls=%fused_computation.278 | loop fusion | flops 7766016 | bytes 11281456 | tf_op jit(solution)/shard_map/sub | solution.py:164
  642.0 5.2 collective-permute-start.61
  648.2 43.4 %while.15 = (s32[]{:T(128)}, f32[3,256,128]{2,1,0:T(8,128)}, s32[12,3]{0,1:T(4,128)S(1)}, f32[12,3,64,64]{3,2,1,0:T(8,128)}, s32[]{:T(128)}) while((s32[]{:T(128)}, f32[3,256,128]{2,1,0:T(8,128)}, s32[12,3]{0,1:T(4,128)S(1)}, f32[12,3,64,64]{3,2,1,0:T(8,128)}, s32[]{:T(128)}) %tuple.132), condition=%wide.while_cond, body=%wide.while_body.sunk | while | flops 2 | bytes 197749 | solution.py:186
  699.5 65.8 %all-reduce.35 = f32[512]{0:T(512)S(1)} all-reduce(f32[512]{0:T(512)S(1)} %select_reduce_fusion), channel_id=2, replica_groups=mesh['gx'=16,'gy'=8] {'gx','gy'}, use_global_device_ids=true, to_apply=%region_5.6.clone | all-reduce | flops 512 | bytes 4096
  (611 shorter events, 375.9 us)
Async XLA Ops:
  1.4 155.5 %collective-permute-start.9 = (f32[3,1,128]{2,1,0:T(1,128)S(1)}, f32[3,1,128]{2,1,0:T(1,128)S(1)}, u32[]{:S(2)}, u32[]{:S(2)}) collective-permute-start(f32[3,1,128]{2,1,0:T(1,128)S(1)} %get-tuple-element.326), channel_id=1, source_target_pairs={{8,0},{16,8},{24,16},{32,24},{40,32},{48,40},{56,48},{64,56},{72,6... | collective-permute-start | bytes 4616 | tf_op jit(solution)/shard_map/ppermute | solution.py:22
  2.8 154.1 %collective-permute-start.8 = (f32[3,1,128]{2,1,0:T(1,128)S(1)}, f32[3,1,128]{2,1,0:T(1,128)S(1)}, u32[]{:S(2)}, u32[]{:S(2)}) collective-permute-start(f32[3,1,128]{2,1,0:T(1,128)S(1)} %get-tuple-element.327), channel_id=1, source_target_pairs={{0,8},{8,16},{16,24},{24,32},{32,40},{40,48},{48,56},{56,64},{64,7... | collective-permute-start | bytes 4616 | tf_op jit(solution)/shard_map/ppermute | solution.py:19
  5.5 161.3 %all-to-all-start = ((s32[128,4,2]{1,2,0:T(2,128)}), s32[128,4,2]{1,2,0:T(2,128)S(1)}, u32[]{:S(2)}, u32[]{:S(2)}) async-start(s32[128,4,2]{1,2,0:T(2,128)} %stack.2), calls=%async_computation | async-start | bytes 262144 | tf_op jit(solution)/shard_map/all_to_all | solution.py:111
  159.9 130.8 %collective-permute-start.11 = (f32[3,258,1]{1,0,2:T(4,128)}, f32[3,258,1]{1,0,2:T(4,128)S(1)}, u32[]{:S(2)}, u32[]{:S(2)}) collective-permute-start(f32[3,258,1]{1,0,2:T(4,128)} %copy.745), channel_id=1, source_target_pairs={{0,1},{1,2},{2,3},{3,4},{4,5},{5,6},{6,7},{7,0},{8,9},{9,10},{10,1... | collective-permute-start | bytes 9296 | tf_op jit(solution)/shard_map/ppermute | solution.py:19
  162.5 129.3 %collective-permute-start.10 = (f32[3,258,1]{1,0,2:T(4,128)}, f32[3,258,1]{1,0,2:T(4,128)}, u32[]{:S(2)}, u32[]{:S(2)}) collective-permute-start(f32[3,258,1]{1,0,2:T(4,128)} %copy.744), channel_id=1, source_target_pairs={{1,0},{2,1},{3,2},{4,3},{5,4},{6,5},{7,6},{0,7},{9,8},{10,9},{11,1... | collective-permute-start | bytes 9296 | tf_op jit(solution)/shard_map/ppermute | solution.py:22
  316.1 6.9 collective-permute-start.17
  320.2 23.0 %collective-permute-start.5 = (f32[3,1,128]{2,1,0:T(1,128)S(1)}, f32[3,1,128]{2,1,0:T(1,128)S(1)}, u32[]{:S(2)}, u32[]{:S(2)}) collective-permute-start(f32[3,1,128]{2,1,0:T(1,128)S(1)} %get-tuple-element.329), channel_id=1, source_target_pairs={{8,0},{16,8},{24,16},{32,24},{40,32},{48,40},{56,48},{64,56},{72,6... | collective-permute-start | bytes 4616 | tf_op jit(solution)/shard_map/ppermute | solution.py:22
  320.8 23.0 %collective-permute-start.4 = (f32[3,1,128]{2,1,0:T(1,128)S(1)}, f32[3,1,128]{2,1,0:T(1,128)}, u32[]{:S(2)}, u32[]{:S(2)}) collective-permute-start(f32[3,1,128]{2,1,0:T(1,128)S(1)} %get-tuple-element.328), channel_id=1, source_target_pairs={{0,8},{8,16},{16,24},{24,32},{32,40},{40,48},{48,56},{56,64},{64,7... | collective-permute-start | bytes 4616 | tf_op jit(solution)/shard_map/ppermute | solution.py:19
  325.7 6.6 collective-permute-start.19
  349.1 6.7 collective-permute-start.23
  363.3 11.3 %collective-permute-start.25 = (f32[3,1,128]{2,0,1:T(4,128)S(1)}, f32[3,1,128]{2,0,1:T(4,128)S(1)}, u32[]{:S(2)}, u32[]{:S(2)}) collective-permute-start(f32[3,1,128]{2,0,1:T(4,128)S(1)} %get-tuple-element.299), channel_id=1, source_target_pairs={{8,0},{16,8},{24,16},{32,24},{40,32},{48,40},{56,48},{64,56},{72,6... | collective-permute-start | bytes 4616 | tf_op jit(solution)/shard_map/ppermute | solution.py:22
  369.0 26.0 %collective-permute-start.7 = (f32[3,258,1]{1,0,2:T(4,128)S(1)}, f32[3,258,1]{1,0,2:T(4,128)S(1)}, u32[]{:S(2)}, u32[]{:S(2)}) collective-permute-start(f32[3,258,1]{1,0,2:T(4,128)S(1)} %copy.741), channel_id=1, source_target_pairs={{1,0},{2,1},{3,2},{4,3},{5,4},{6,5},{7,6},{0,7},{9,8},{10,9},{11,1... | collective-permute-start | bytes 9296 | tf_op jit(solution)/shard_map/ppermute | solution.py:22
  374.6 21.6 %collective-permute-start.6 = (f32[3,258,1]{1,0,2:T(4,128)S(1)}, f32[3,258,1]{1,0,2:T(4,128)S(1)}, u32[]{:S(2)}, u32[]{:S(2)}) collective-permute-start(f32[3,258,1]{1,0,2:T(4,128)S(1)} %copy.740), channel_id=1, source_target_pairs={{0,1},{1,2},{2,3},{3,4},{4,5},{5,6},{6,7},{7,0},{8,9},{9,10},{10,1... | collective-permute-start | bytes 9296 | tf_op jit(solution)/shard_map/ppermute | solution.py:19
  398.3 7.4 collective-permute-start.30
  415.2 12.9 %collective-permute-start.1 = (f32[9,1,128]{2,0,1:T(8,128)S(1)}, f32[9,1,128]{2,0,1:T(8,128)S(1)}, u32[]{:S(2)}, u32[]{:S(2)}) collective-permute-start(f32[9,1,128]{2,0,1:T(8,128)S(1)} %get-tuple-element.233), channel_id=1, source_target_pairs={{8,0},{16,8},{24,16},{32,24},{40,32},{48,40},{56,48},{64,56},{72,6... | collective-permute-start | bytes 13832 | tf_op jit(solution)/shard_map/ppermute | solution.py:22
  417.2 10.9 %collective-permute-start = (f32[9,1,128]{2,0,1:T(8,128)S(1)}, f32[9,1,128]{2,0,1:T(8,128)S(1)}, u32[]{:S(2)}, u32[]{:S(2)}) collective-permute-start(f32[9,1,128]{2,0,1:T(8,128)S(1)} %get-tuple-element.232), channel_id=1, source_target_pairs={{0,8},{8,16},{16,24},{24,32},{32,40},{40,48},{48,56},{56,64},{64,7... | collective-permute-start | bytes 13832 | tf_op jit(solution)/shard_map/ppermute | solution.py:19
  421.1 19.7 %collective-permute-start.35 = (f32[3,258,1]{1,0,2:T(4,128)S(1)}, f32[3,258,1]{1,0,2:T(4,128)}, u32[]{:S(2)}, u32[]{:S(2)}) collective-permute-start(f32[3,258,1]{1,0,2:T(4,128)S(1)} %copy.696), channel_id=1, source_target_pairs={{0,1},{1,2},{2,3},{3,4},{4,5},{5,6},{6,7},{7,0},{8,9},{9,10},{10,1... | collective-permute-start | bytes 9296 | tf_op jit(solution)/shard_map/ppermute | solution.py:19
  423.0 19.5 %collective-permute-start.34 = (f32[3,258,1]{1,0,2:T(4,128)}, f32[3,258,1]{1,0,2:T(4,128)}, u32[]{:S(2)}, u32[]{:S(2)}) collective-permute-start(f32[3,258,1]{1,0,2:T(4,128)} %copy.694), channel_id=1, source_target_pairs={{1,0},{2,1},{3,2},{4,3},{5,4},{6,5},{7,6},{0,7},{9,8},{10,9},{11,1... | collective-permute-start | bytes 9296 | tf_op jit(solution)/shard_map/ppermute | solution.py:22
  434.0 10.4 %collective-permute-start.3 = (f32[9,258,1]{1,0,2:T(8,128)S(1)}, f32[9,258,1]{1,0,2:T(8,128)S(1)}, u32[]{:S(2)}, u32[]{:S(2)}) collective-permute-start(f32[9,258,1]{1,0,2:T(8,128)S(1)} %copy.628), channel_id=1, source_target_pairs={{1,0},{2,1},{3,2},{4,3},{5,4},{6,5},{7,6},{0,7},{9,8},{10,9},{11,1... | collective-permute-start | bytes 27872 | tf_op jit(solution)/shard_map/ppermute | solution.py:22
  439.2 7.8 %collective-permute-start.2 = (f32[9,258,1]{1,0,2:T(8,128)S(1)}, f32[9,258,1]{1,0,2:T(8,128)S(1)}, u32[]{:S(2)}, u32[]{:S(2)}) collective-permute-start(f32[9,258,1]{1,0,2:T(8,128)S(1)} %copy.627), channel_id=1, source_target_pairs={{0,1},{1,2},{2,3},{3,4},{4,5},{5,6},{6,7},{7,0},{8,9},{9,10},{10,1... | collective-permute-start | bytes 27872 | tf_op jit(solution)/shard_map/ppermute | solution.py:19
  475.8 9.3 %collective-permute-start.39 = (f32[3,258,1]{1,0,2:T(4,128)}, f32[3,258,1]{1,0,2:T(4,128)}, u32[]{:S(2)}, u32[]{:S(2)}) collective-permute-start(f32[3,258,1]{1,0,2:T(4,128)} %copy.703), channel_id=1, source_target_pairs={{1,0},{2,1},{3,2},{4,3},{5,4},{6,5},{7,6},{0,7},{9,8},{10,9},{11,1... | collective-permute-start | bytes 9296 | tf_op jit(solution)/shard_map/ppermute | solution.py:22
  482.4 6.8 collective-permute-start.38
  495.2 6.8 collective-permute-start.41
  506.5 7.1 collective-permute-start.43
  533.4 7.3 collective-permute-start.47
  562.1 7.1 collective-permute-start.51
  589.3 7.3 collective-permute-start.55
  616.1 7.2 collective-permute-start.59
  642.0 51.5 %collective-permute-start.61 = (f32[3,1,128]{2,0,1:T(4,128)S(1)}, f32[3,1,128]{2,0,1:T(4,128)S(1)}, u32[]{:S(2)}, u32[]{:S(2)}) collective-permute-start(f32[3,1,128]{2,0,1:T(4,128)S(1)} %get-tuple-element.263), channel_id=1, source_target_pairs={{8,0},{16,8},{24,16},{32,24},{40,32},{48,40},{56,48},{64,56},{72,6... | collective-permute-start | bytes 4616 | tf_op jit(solution)/shard_map/ppermute | solution.py:22
  647.2 46.3 %collective-permute-start.60 = (f32[3,1,128]{2,0,1:T(4,128)S(1)}, f32[3,1,128]{2,0,1:T(4,128)S(1)}, u32[]{:S(2)}, u32[]{:S(2)}) collective-permute-start(f32[3,1,128]{2,0,1:T(4,128)S(1)} %get-tuple-element.262), channel_id=1, source_target_pairs={{0,8},{8,16},{16,24},{24,32},{32,40},{40,48},{48,56},{56,64},{64,7... | collective-permute-start | bytes 4616 | tf_op jit(solution)/shard_map/ppermute | solution.py:19
  696.1 69.8 %collective-permute-start.63 = (f32[3,258,1]{1,0,2:T(4,128)S(1)}, f32[3,258,1]{1,0,2:T(4,128)S(1)}, u32[]{:S(2)}, u32[]{:S(2)}) collective-permute-start(f32[3,258,1]{1,0,2:T(4,128)S(1)} %copy.733), channel_id=1, source_target_pairs={{1,0},{2,1},{3,2},{4,3},{5,4},{6,5},{7,6},{0,7},{9,8},{10,9},{11,1... | collective-permute-start | bytes 9296 | tf_op jit(solution)/shard_map/ppermute | solution.py:22
  698.3 68.6 %collective-permute-start.62 = (f32[3,258,1]{1,0,2:T(4,128)S(1)}, f32[3,258,1]{1,0,2:T(4,128)S(1)}, u32[]{:S(2)}, u32[]{:S(2)}) collective-permute-start(f32[3,258,1]{1,0,2:T(4,128)S(1)} %copy.732), channel_id=1, source_target_pairs={{0,1},{1,2},{2,3},{3,4},{4,5},{5,6},{6,7},{7,0},{8,9},{9,10},{10,1... | collective-permute-start | bytes 9296 | tf_op jit(solution)/shard_map/ppermute | solution.py:19
  (143 other events, 1137.6 us)
